TPU v7x, 32 devices: a whole 2x2x4 slice. The times are simulated.
32 devices in a mesh: batch: 8 (over y, x, core), mp: 4 (over z).
Axes of the slice: x: 2, y: 2, z: 4, core: 2. Of those that a mesh axis runs over, the one named last changes fastest.
Arguments:
- token_ids: int32 [8, 1536], P('batch'), may hold values from 0 to 30527
- segment_ids: int32 [8, 1536], P('batch'), may hold values from 0 to 8, never falling along the last dimension, each value on 1 to 1024 neighbouring positions
- row_of: int32 [30528], replicated, may hold values from 0 to 30527, each once
- query_count: int32 [1], replicated, may hold values from 16 to 32
- table: float32 [30528, 768], P('batch'), may hold values from -8 to 8
- qkv_weight: float32 [768, 3, 768], P('batch', None, 'mp'), may hold values from -0.21875 to 0.21875
- out_weight: float32 [768, 768], P('mp', 'batch'), may hold values from -0.875 to 0.875
- gate_up_weight: float32 [768, 2, 3072], P('batch', None, 'mp'), may hold values from -0.21875 to 0.21875
- down_weight: float32 [3072, 768], P('mp', 'batch'), may hold values from -0.109375 to 0.109375
- gains: float32 [2, 768], P(None, 'batch'), may hold values from 0.3 to 2.5
- table_m: float32 [30528, 768], P('batch'), may hold values from -0.0009765625 to 0.0009765625
- qkv_m: float32 [768, 3, 768], P('batch', None, 'mp'), may hold values from -0.0009765625 to 0.0009765625
- out_m: float32 [768, 768], P('mp', 'batch'), may hold values from -0.0009765625 to 0.0009765625
- gate_up_m: float32 [768, 2, 3072], P('batch', None, 'mp'), may hold values from -0.0009765625 to 0.0009765625
- down_m: float32 [3072, 768], P('mp', 'batch'), may hold values from -0.0009765625 to 0.0009765625
- gains_m: float32 [2, 768], P(None, 'batch'), may hold values from -0.0009765625 to 0.0009765625
- table_v: float32 [30528, 768], P('batch'), may hold values from 3.040972e-08 to 1.2163888e-07
- qkv_v: float32 [768, 3, 768], P('batch', None, 'mp'), may hold values from 3.040972e-08 to 1.2163888e-07
- out_v: float32 [768, 768], P('mp', 'batch'), may hold values from 3.040972e-08 to 1.2163888e-07
- gate_up_v: float32 [768, 2, 3072], P('batch', None, 'mp'), may hold values from 3.040972e-08 to 1.2163888e-07
- down_v: float32 [3072, 768], P('mp', 'batch'), may hold values from 3.040972e-08 to 1.2163888e-07
- gains_v: float32 [2, 768], P(None, 'batch'), may hold values from 3.040972e-08 to 1.2163888e-07
Outputs:
- loss: float32 [1], replicated
- grad_norm: float32 [1], replicated
- new_table: float32 [30528, 768], P('batch')
- new_qkv_weight: float32 [768, 3, 768], P('batch', None, 'mp')
- new_out_weight: float32 [768, 768], P('mp', 'batch')
- new_gate_up_weight: float32 [768, 2, 3072], P('batch', None, 'mp')
- new_down_weight: float32 [3072, 768], P('mp', 'batch')
- new_gains: float32 [2, 768], P(None, 'batch')
- clipped_table_grad: float32 [30528, 768], P('batch')
- new_qkv_m: float32 [768, 3, 768], P('batch', None, 'mp')
- new_out_m: float32 [768, 768], P('mp', 'batch')
- new_gate_up_m: float32 [768, 2, 3072], P('batch', None, 'mp')
- new_down_m: float32 [3072, 768], P('mp', 'batch')
- new_gains_m: float32 [2, 768], P(None, 'batch')
- new_table_v: float32 [30528, 768], P('batch')
- new_qkv_v: float32 [768, 3, 768], P('batch', None, 'mp')
- new_out_v: float32 [768, 768], P('mp', 'batch')
- new_gate_up_v: float32 [768, 2, 3072], P('batch', None, 'mp')
- new_down_v: float32 [3072, 768], P('mp', 'batch')
- new_gains_v: float32 [2, 768], P(None, 'batch')
Inputs may be any that keep to these rules, and one draw needn't show every extreme that they name: `segment_ids`: in each row the ids never fall, every id 0 to 8 appears, id 8 marks padding, each segment has 1 to 1024 tokens and one has exactly 1024. A permutation: token t's embedding is table row row_of[t]. The first query_count queries count.
All inputs are finite; a program needn't handle non-finite values.
Results may differ from a plain program's by a relative error of at most 0.0075.
The roundings to bfloat16 on the way count: a program that leaves them out, or rounds other values in their place, can miss the bound.
Values may be sent and summed in bfloat16 or wider, within the bound.
A program may use at most 320 MiB of HBM per device.

v0:
```python
from functools import partial
import jax
import jax.numpy as jnp
from jax import lax
from jax.sharding import PartitionSpec as P

D = 768
HEAD_DIM = 64
SEGS = 8
peak_affinity = lax.Precision.HIGHEST
sharpness_divisor = 0.05
clip_limit = 1.0
step_number = 3.0
rates = (0.3, 0.02, 0.02, 0.02, 0.02, 0.3)
negative = -1e30


def positions(segment_row, segment_count):
    labels = jnp.arange(segment_count + 1, dtype=jnp.int32)
    member = (segment_row[:, None] == labels[None, :]).astype(jnp.int32)
    counts = jnp.sum(member, 0)
    starts = jnp.cumsum(counts) - counts
    first_index = jnp.sum(member * starts[None, :], 1)
    return (jnp.arange(segment_row.shape[0], dtype=jnp.int32) - first_index).astype(jnp.float32)


def rotate(values, places):
    half_dim = values.shape[-1] // 2
    freqs = jnp.power(1000.0, -2.0 * jnp.arange(half_dim, dtype=jnp.float32) / values.shape[-1])
    angles = places[:, None] * freqs[None, :]
    cosine = jnp.cos(angles)[:, None, :]
    sine = jnp.sin(angles)[:, None, :]
    former = values[..., :half_dim]
    latter = values[..., half_dim:]
    return jnp.concatenate([former * cosine - latter * sine, latter * cosine + former * sine], -1)


def layer_norm(values, gain):
    centred = values - jnp.mean(values, -1, keepdims=True)
    spread = jnp.mean(centred * centred, -1, keepdims=True)
    return centred * lax.rsqrt(spread + 1e-05) * gain


def swiglu(gate_up):
    return jax.nn.silu(gate_up[:, 0]) * gate_up[:, 1]


def contract(left, right, left_dim, right_dim):
    return lax.dot_general(
        left, right, (((left_dim,), (right_dim,)), ((), ())), preferred_element_type=jnp.float32
    )


def pool_rows(hidden, segment_ids):
    rows_dev, length = segment_ids.shape
    labels = jnp.arange(SEGS, dtype=jnp.int32)
    member = (segment_ids[:, None, :] == labels[None, :, None]).astype(jnp.float32)
    sums = jnp.einsum(
        "rsl,rld->rsd", member, hidden.reshape(rows_dev, length, -1), precision=peak_affinity
    )
    pooled = (sums / jnp.sum(member, -1, keepdims=True)).reshape(rows_dev * SEGS, -1)
    return pooled * lax.rsqrt(jnp.sum(pooled * pooled, -1, keepdims=True) + 1e-06)


def block_scores(query_block, key_row, segment_block, segment_row):
    scores = jnp.einsum(
        "qhd,khd->hqk", query_block, key_row, preferred_element_type=jnp.float32
    ) * HEAD_DIM ** (-0.5)
    same = segment_block[:, None] == segment_row[None, :]
    return jnp.where(same[None], scores, negative)


def attend(query, keys, values, segment_ids, width):
    rows_dev, length = segment_ids.shape
    per_row = length // width
    flat_segments = segment_ids.reshape(-1)

    def one_block(block):
        row_index = block // per_row
        query_block = lax.dynamic_slice_in_dim(query, block * width, width, 0)
        segment_block = lax.dynamic_slice_in_dim(flat_segments, block * width, width, 0)
        scores = block_scores(query_block, keys[row_index], segment_block, segment_ids[row_index])
        peak_score = jnp.max(scores, -1, keepdims=True)
        weights = jnp.exp(scores - peak_score)
        totals = jnp.sum(weights, -1, keepdims=True)
        probs = (weights / totals).astype(jnp.bfloat16)
        output = jnp.einsum(
            "hqk,khd->qhd", probs, values[row_index], preferred_element_type=jnp.float32
        )
        return (output, (peak_score + jnp.log(totals))[..., 0])

    outputs, log_totals = lax.map(one_block, jnp.arange(rows_dev * per_row, dtype=jnp.int32))
    return (outputs.reshape((rows_dev * length,) + outputs.shape[2:]), log_totals)


def attend_back(query, keys, values, segment_ids, log_totals, grad_out, width):
    rows_dev, length = segment_ids.shape
    per_row = length // width
    flat_segments = segment_ids.reshape(-1)
    factor = HEAD_DIM ** (-0.5)

    def one_block(carry, block):
        grad_keys, grad_values = carry
        row_index = block // per_row
        query_block = lax.dynamic_slice_in_dim(query, block * width, width, 0)
        segment_block = lax.dynamic_slice_in_dim(flat_segments, block * width, width, 0)
        grad_block = lax.dynamic_slice_in_dim(grad_out, block * width, width, 0)
        scores = block_scores(query_block, keys[row_index], segment_block, segment_ids[row_index])
        probs = jnp.exp(scores - log_totals[block][..., None])
        grad_probs = jnp.einsum(
            "qhd,khd->hqk", grad_block, values[row_index], preferred_element_type=jnp.float32
        )
        inner = jnp.sum(probs * grad_probs, -1, keepdims=True)
        grad_scores = (probs * (grad_probs - inner)).astype(jnp.bfloat16)
        grad_query = (
            jnp.einsum(
                "hqk,khd->qhd", grad_scores, keys[row_index], preferred_element_type=jnp.float32
            )
            * factor
        )
        key_term = (
            jnp.einsum("hqk,qhd->khd", grad_scores, query_block, preferred_element_type=jnp.float32)
            * factor
        )
        value_term = jnp.einsum(
            "hqk,qhd->khd",
            probs.astype(jnp.bfloat16),
            grad_block,
            preferred_element_type=jnp.float32,
        )
        return (
            (grad_keys.at[row_index].add(key_term), grad_values.at[row_index].add(value_term)),
            grad_query,
        )

    zeros = jnp.zeros(keys.shape, jnp.float32)
    (grad_keys, grad_values), grad_query = lax.scan(
        one_block, (zeros, zeros), jnp.arange(rows_dev * per_row, dtype=jnp.int32)
    )
    return (grad_query.reshape((rows_dev * length,) + grad_query.shape[2:]), grad_keys, grad_values)


def adam_update(weight, grad, first, second, rate):
    first = 0.5 * first + 0.5 * grad
    second = 0.5 * second + 0.5 * grad * grad
    correction = 1.0 - 0.5**step_number
    weight = weight - rate * (
        first / correction / (jnp.sqrt(second / correction) + 1e-08) + 0.01 * weight
    )
    return (weight, first, second)


def local(
    token_ids,
    segment_ids,
    row_of,
    query_count,
    table,
    qkv_weight,
    out_weight,
    gate_up_weight,
    down_weight,
    gains,
    table_m,
    qkv_m,
    out_m,
    gate_up_m,
    down_m,
    gains_m,
    table_v,
    qkv_v,
    out_v,
    gate_up_v,
    down_v,
    gains_v,
):
    local_width = table.shape[1] // lax.axis_size("mp")
    column = lax.axis_index("mp") * local_width
    table_cols = lax.dynamic_slice_in_dim(table, column, local_width, 1)
    low_table, w_qkv, w_out, w_gu, w_down, gain_low = (
        lax.all_gather(table_cols.astype(jnp.bfloat16), "batch", axis=0, tiled=True),
        lax.all_gather(qkv_weight.astype(jnp.bfloat16), "batch", axis=0, tiled=True),
        lax.all_gather(out_weight.astype(jnp.bfloat16), "batch", axis=1, tiled=True),
        lax.all_gather(gate_up_weight.astype(jnp.bfloat16), "batch", axis=0, tiled=True),
        lax.all_gather(down_weight.astype(jnp.bfloat16), "batch", axis=1, tiled=True),
        lax.all_gather(gains.astype(jnp.bfloat16), "batch", axis=1, tiled=True),
    )
    gain = gain_low.astype(jnp.float32)
    rows_dev, length = token_ids.shape
    tokens = rows_dev * length
    width = min(512, length)
    heads_local = w_qkv.shape[2] // HEAD_DIM
    ff_local = w_gu.shape[2]
    table_rows = row_of[token_ids.reshape(-1)]
    x_zero = lax.all_gather(low_table[table_rows], "mp", axis=1, tiled=True)
    places = jax.vmap(partial(positions, segment_count=SEGS))(segment_ids).reshape(-1)
    qkv = jnp.dot(x_zero, w_qkv.reshape(D, -1), preferred_element_type=jnp.float32).reshape(
        tokens, 3, heads_local, HEAD_DIM
    )
    query = rotate(qkv[:, 0], places).astype(jnp.bfloat16)
    keys = (
        rotate(qkv[:, 1], places)
        .astype(jnp.bfloat16)
        .reshape(rows_dev, length, heads_local, HEAD_DIM)
    )
    values = qkv[:, 2].astype(jnp.bfloat16).reshape(rows_dev, length, heads_local, HEAD_DIM)
    attended, log_totals = attend(query, keys, values, segment_ids, width)
    attended_low = attended.reshape(tokens, -1).astype(jnp.bfloat16)
    attn_term = jnp.dot(attended_low, w_out, preferred_element_type=jnp.float32)
    attn = lax.psum(attn_term, "mp")
    hidden_one, first_back = jax.vjp(layer_norm, x_zero.astype(jnp.float32) + attn, gain[0])
    hidden_low = hidden_one.astype(jnp.bfloat16)
    gate_up = jnp.dot(hidden_low, w_gu.reshape(D, -1), preferred_element_type=jnp.float32).reshape(
        tokens, 2, ff_local
    )
    active, swiglu_back = jax.vjp(swiglu, gate_up)
    active_low = active.astype(jnp.bfloat16)
    mlp = lax.psum(jnp.dot(active_low, w_down, preferred_element_type=jnp.float32), "mp")
    hidden_two, second_back = jax.vjp(layer_norm, hidden_one + mlp, gain[1])
    embed, pool_back = jax.vjp(lambda hidden: pool_rows(hidden, segment_ids), hidden_two)
    batch_index = lax.axis_index("batch")
    half_count = lax.axis_size("batch") // 2
    texts = embed.shape[0]
    queries_all = half_count * texts
    everyone = lax.all_gather(embed, "batch", axis=0, tiled=True)
    question_vectors = everyone[:queries_all]
    passage_vectors = everyone[queries_all:]
    limit = query_count[0].astype(jnp.float32)
    labels = jnp.arange(queries_all, dtype=jnp.int32)
    weight_rows = (labels < query_count[0]).astype(jnp.float32) / limit
    affinity_scores = (
        jnp.dot(question_vectors, passage_vectors.T, precision=peak_affinity) / sharpness_divisor
    )
    target = (labels[:, None] == labels[None, :]).astype(jnp.float32)
    loss_value = jnp.sum(
        weight_rows
        * (jax.nn.logsumexp(affinity_scores, -1) - jnp.sum(affinity_scores * target, -1))
    )
    affinity_derivative = (jax.nn.softmax(affinity_scores, -1) - target) * weight_rows[:, None]
    grad_all = jnp.concatenate(
        [
            jnp.dot(affinity_derivative, passage_vectors, precision=peak_affinity)
            / sharpness_divisor,
            jnp.dot(affinity_derivative.T, question_vectors, precision=peak_affinity)
            / sharpness_divisor,
        ],
        0,
    )
    grad_embed = lax.dynamic_slice_in_dim(grad_all, batch_index * texts, texts, 0)
    (grad_two,) = pool_back(grad_embed)
    grad_second, grad_gain_two = second_back(grad_two)
    grad_mlp_low = grad_second.astype(jnp.bfloat16)
    grad_active = contract(grad_mlp_low, w_down, 1, 1)
    grad_down = contract(active_low, grad_mlp_low, 0, 0)
    (grad_gate_up,) = swiglu_back(grad_active)
    grad_gu_low = grad_gate_up.reshape(tokens, -1).astype(jnp.bfloat16)
    back_term = contract(grad_gu_low, w_gu.reshape(D, -1), 1, 1)
    grad_one = grad_second + lax.psum(back_term, "mp")
    grad_first, grad_gain_one = first_back(grad_one)
    grad_gu = contract(hidden_low, grad_gu_low, 0, 0)
    grad_attn_low = grad_first.astype(jnp.bfloat16)
    grad_attended = contract(grad_attn_low, w_out, 1, 1).astype(jnp.bfloat16)
    grad_out = contract(attended_low, grad_attn_low, 0, 0)
    grad_query, grad_keys, grad_values = attend_back(
        query,
        keys,
        values,
        segment_ids,
        log_totals,
        grad_attended.reshape(tokens, heads_local, HEAD_DIM),
        width,
    )
    _, rotate_back = jax.vjp(lambda inputs: rotate(inputs, places), qkv[:, 0])
    (grad_query_raw,) = rotate_back(grad_query)
    (grad_key_raw,) = rotate_back(grad_keys.reshape(tokens, heads_local, HEAD_DIM))
    grad_qkv_low = (
        jnp.stack(
            [grad_query_raw, grad_key_raw, grad_values.reshape(tokens, heads_local, HEAD_DIM)], 1
        )
        .reshape(tokens, -1)
        .astype(jnp.bfloat16)
    )
    grad_zero = grad_first + lax.psum(contract(grad_qkv_low, w_qkv.reshape(D, -1), 1, 1), "mp")
    grad_qkv = contract(x_zero, grad_qkv_low, 0, 0)
    grad_table = (
        jnp.zeros((low_table.shape[0], local_width), jnp.float32)
        .at[table_rows]
        .add(lax.dynamic_slice_in_dim(grad_zero, column, local_width, 1))
    )
    grad_gains = jnp.stack([grad_gain_one, grad_gain_two], 0)
    reduced = (
        lax.psum_scatter(grad_table, "batch", scatter_dimension=0, tiled=True),
        lax.psum_scatter(grad_qkv.reshape(D, 3, -1), "batch", scatter_dimension=0, tiled=True),
        lax.psum_scatter(grad_out, "batch", scatter_dimension=1, tiled=True),
        lax.psum_scatter(grad_gu.reshape(D, 2, -1), "batch", scatter_dimension=0, tiled=True),
        lax.psum_scatter(grad_down, "batch", scatter_dimension=1, tiled=True),
        lax.psum_scatter(grad_gains, "batch", scatter_dimension=1, tiled=True),
    )
    squares = sum((jnp.sum(part * part) for part in reduced[:5])) + jnp.sum(
        reduced[5] * reduced[5]
    ) / lax.axis_size("mp")
    table_full = lax.all_gather(reduced[0], "mp", axis=1, tiled=True)
    total_squares = lax.psum(squares, ("batch", "mp"))
    grad_norm = jnp.sqrt(total_squares)
    scale = clip_limit / jnp.maximum(grad_norm, clip_limit)
    olds = (table, qkv_weight, out_weight, gate_up_weight, down_weight, gains)
    grads_all = (table_full,) + tuple(reduced[1:])
    firsts = (table_m, qkv_m, out_m, gate_up_m, down_m, gains_m)
    seconds = (table_v, qkv_v, out_v, gate_up_v, down_v, gains_v)
    updated = [
        adam_update(weight_old, grad_part * scale, first_old, second_old, rate)
        for weight_old, grad_part, first_old, second_old, rate in zip(
            olds, grads_all, firsts, seconds, rates
        )
    ]
    clipped_table = table_full * scale
    loss = loss_value.reshape(1)
    return (
        loss,
        grad_norm.reshape(1),
        updated[0][0],
        updated[1][0],
        updated[2][0],
        updated[3][0],
        updated[4][0],
        updated[5][0],
        clipped_table,
        updated[1][1],
        updated[2][1],
        updated[3][1],
        updated[4][1],
        updated[5][1],
        updated[0][2],
        updated[1][2],
        updated[2][2],
        updated[3][2],
        updated[4][2],
        updated[5][2],
    )


def solution(mesh):
    placed = (
        P("batch", None),
        P("batch", None),
        P(),
        P(),
        P("batch", None),
        P("batch", None, "mp"),
        P("mp", "batch"),
        P("batch", None, "mp"),
        P("mp", "batch"),
        P(None, "batch"),
        P("batch", None),
        P("batch", None, "mp"),
        P("mp", "batch"),
        P("batch", None, "mp"),
        P("mp", "batch"),
        P(None, "batch"),
        P("batch", None),
        P("batch", None, "mp"),
        P("mp", "batch"),
        P("batch", None, "mp"),
        P("mp", "batch"),
        P(None, "batch"),
    )
    return jax.shard_map(
        local,
        mesh=mesh,
        in_specs=placed,
        out_specs=(
            P(),
            P(),
            P("batch", None),
            P("batch", None, "mp"),
            P("mp", "batch"),
            P("batch", None, "mp"),
            P("mp", "batch"),
            P(None, "batch"),
            P("batch", None),
            P("batch", None, "mp"),
            P("mp", "batch"),
            P("batch", None, "mp"),
            P("mp", "batch"),
            P(None, "batch"),
            P("batch", None),
            P("batch", None, "mp"),
            P("mp", "batch"),
            P("batch", None, "mp"),
            P("mp", "batch"),
            P(None, "batch"),
        ),
        check_vma=False,
    )
```

profile of v0, /device:TPU:0, one launch (start us, length us, event | category | flops | bytes accessed | tf_op | source)
XLA Modules:
  0.0 1895.6 jit_solution(3074774490312549609)
XLA Ops:
  7.3 12.4 copy.141
  22.9 8.4 gather_fusion
  31.4 63.1 %all-gather.17.cloned.1.call-done = bf16[8,3816,192]{1,2,0:T(8,128)(2,1)} async-done(((bf16[1,3816,192]{1,2,0:T(8,128)(2,1)}), bf16[8,3816,192]{1,2,0:T(8,128)(2,1)}) %all-gather.17.cloned.1.call-update) | async-done | bytes 11722768 | tf_op jit(solution)/shard_map/all_gather | solution.py:181
  94.5 18.1 copy.142
  112.6 11.2 gather_fusion.1
  126.6 13.2 all_gather.29
  141.9 9.2 all_gather.30
  151.9 23.6 %all-gather.15.cloned.1.call-done = bf16[1536,768]{0,1:T(8,128)(2,1)} async-done(((bf16[1536,192]{0,1:T(8,128)(2,1)}), bf16[1536,768]{0,1:T(8,128)(2,1)}) %all-gather.15.cloned.1.call-update) | async-done | bytes 2359312 | tf_op jit(solution)/shard_map/all_gather | solution.py:195
  179.8 33.9 %while.31 = (s32[]{:T(128)}, bf16[3,512,3,64]{1,3,2,0:T(8,128)(2,1)}, f32[3,3,512]{2,1,0:T(4,128)S(1)}, s32[3]{0:T(128)S(1)}, s32[1536]{0:T(1024)S(1)}, /*index=...) while((s32[]{:T(128)}, ...), condition=%wide.region_6.7_spmd, body=%wide.region_3.6_spmd.sunk | while | flops 633076224 | bytes 38029568 | solution.py:92
  219.3 8.9 all-gather.2
  232.6 156.8 %all-reduce.11.cloned.1.call-done = f32[1536,768]{0,1:T(8,128)} async-done(((f32[1536,768]{0,1:T(8,128)}), f32[1536,768]{0,1:T(8,128)}) %all-reduce.11.cloned.1.call-update) | async-done | bytes 4718608 | tf_op jit(solution)/shard_map/psum | solution.py:210
  407.1 7.7 all-gather.11.cloned.1.call-done
  414.8 6.2 fusion.123
  421.9 171.2 %all-reduce.13.cloned.1.call-done = f32[1536,768]{0,1:T(8,128)} async-done(((f32[1536,768]{0,1:T(8,128)}), f32[1536,768]{0,1:T(8,128)}) %all-reduce.13.cloned.1.call-update) | async-done | bytes 4718608 | tf_op jit(solution)/shard_map/psum | solution.py:218
  601.2 9.5 all_gather.34
  625.3 7.9 convolution_bitcast_fusion
  633.7 169.7 %all-reduce.15.cloned.1.call-done = f32[1536,768]{0,1:T(8,128)} async-done(((f32[1536,768]{0,1:T(8,128)}), f32[1536,768]{0,1:T(8,128)}) %all-reduce.15.cloned.1.call-update) | async-done | bytes 4718608 | tf_op jit(solution)/shard_map/psum | solution.py:258
  803.4 6.2 multiply_reduce_fusion.2
  821.4 161.7 %while.32 = (s32[]{:T(128)}, f32[1,1536,3,64]{1,3,2,0:T(8,128)}, f32[1,1536,3,64]{1,3,2,0:T(8,128)S(1)}, f32[3,512,3,64]{1,0,3,2:T(4,128)}, s32[3]{0:T(128)S(1)}...) while((s32[]{:T(128)}, f32[1,1536,3,64]{1,3,2,0:T(8,128)}, ...), condition=%wide.region_29.30_spmd.clone, body=%wide.region_26.29_spmd.clone.sunk | while | flops 1534130688 | bytes 86367704 | solution.py:137
  831.3 8.1 multiply_reduce_fusion.16
  839.3 9.4 multiply_convert_fusion.4
  853.0 8.6 dynamic_update_slice.22
  876.3 6.1 fusion.167
  885.0 8.1 multiply_reduce_fusion.16
  893.0 9.4 multiply_convert_fusion.4
  906.7 8.6 dynamic_update_slice.22
  930.4 6.1 fusion.167
  939.0 8.1 multiply_reduce_fusion.16
  947.1 9.4 multiply_convert_fusion.4
  960.7 8.6 dynamic_update_slice.22
  993.0 171.1 %all-reduce.17.cloned.1.call-done = f32[1536,768]{0,1:T(8,128)} async-done(((f32[1536,768]{0,1:T(8,128)}), f32[1536,768]{0,1:T(8,128)}) %all-reduce.17.cloned.1.call-update) | async-done | bytes 4718608 | tf_op jit(solution)/shard_map/psum | solution.py:283
  1166.3 21.2 %scatter_custom_fusion = f32[30528,192]{1,0:T(8,128)} fusion(s32[1536]{0:T(1024)} %copy-done.49, f32[1536,192]{1,0:T(8,128)S(1)} %copy.157, f32[]{:T(128)} %constant.228.clone.1), kind=kCustom, calls=%fused_computation.51 | custom fusion | flops 294912 | bytes 23446016 | tf_op jit(solution)/shard_map/scatter-add | solution.py:288
  1201.7 15.3 fusion.50
  1224.7 151.4 %reduce-scatter.11.cloned.1.call-done = f32[3816,192]{1,0:T(8,128)} async-done(((f32[30528,192]{1,0:T(8,128)}), f32[3816,192]{1,0:T(8,128)}) %reduce-scatter.11.cloned.1.call-update) | async-done | bytes 2930704 | tf_op jit(solution)/shard_map/reduce_scatter | solution.py:292
  1381.2 12.6 copy.160
  1393.8 28.0 %reduce-scatter.17.cloned.1.call-done = f32[768,96]{0,1:T(8,128)} async-done(((f32[768,768]{0,1:T(8,128)}), f32[768,96]{0,1:T(8,128)}) %reduce-scatter.17.cloned.1.call-update) | async-done | bytes 294928 | tf_op jit(solution)/shard_map/reduce_scatter | solution.py:296
  1423.5 36.1 %reduce-scatter.21.cloned.1.call-done = f32[96,2]{1,0:T(8,128)} async-done(((f32[768,2]{1,0:T(8,128)}), f32[96,2]{1,0:T(8,128)}) %reduce-scatter.21.cloned.1.call-update) | async-done | bytes 784
  1461.8 36.2 %reduce-scatter.19.cloned.1.call-done = f32[96,192]{1,0:T(8,128)} async-done(((f32[768,192]{1,0:T(8,128)}), f32[96,192]{1,0:T(8,128)}) %reduce-scatter.19.cloned.1.call-update) | async-done | bytes 73744
  1499.6 56.7 %reduce-scatter.15.cloned.1.call-done = f32[96,2,768]{2,0,1:T(8,128)} async-done(((f32[768,2,768]{2,0,1:T(8,128)}), f32[96,2,768]{2,0,1:T(8,128)}) %reduce-scatter.15.cloned.1.call-update) | async-done | bytes 589840 | tf_op jit(solution)/shard_map/reduce_scatter | solution.py:295
  1558.1 44.5 %reduce-scatter.13.cloned.1.call-done = f32[96,3,192]{2,0,1:T(8,128)} async-done(((f32[768,3,192]{2,0,1:T(8,128)}), f32[96,3,192]{2,0,1:T(8,128)}) %reduce-scatter.13.cloned.1.call-update) | async-done | bytes 221200 | tf_op jit(solution)/shard_map/reduce_scatter | solution.py:293
  1611.3 13.3 copy.158
  1624.7 53.5 %psum.39 = f32[]{:T(128)} all-reduce(f32[]{:T(128)S(6)} %add.324), channel_id=1, replica_groups=mesh['batch'=8,'mp'=4] {'batch','mp'}, use_global_device_ids=true, to_apply=%region_46.47 | all-reduce | flops 1 | bytes 8 | tf_op jit(solution)/shard_map/psum | solution.py:303
  1687.7 123.4 %all-gather.13.cloned.1.call-done = f32[3816,768]{0,1:T(8,128)} async-done(((f32[3816,192]{0,1:T(8,128)}), f32[3816,768]{0,1:T(8,128)}) %all-gather.13.cloned.1.call-update) | async-done | bytes 11722768 | tf_op jit(solution)/shard_map/all_gather | solution.py:302
  1811.0 17.3 fusion.46
  1828.4 12.3 copy.169
  1840.7 22.2 %fusion.45 = f32[3816,768]{0,1:T(8,128)} fusion(f32[3816,768]{0,1:T(8,128)} %copy.141, f32[3816,768]{0,1:T(8,128)} %get-tuple-element.440, f32[3816,768]{0,1:T(8,128)} %copy.158, f32[3816,768]{0,1:T(8,128)} %copy.160), kind=kLoop, calls=%fused_computation.57 | loop fusion | flops 41029632 | bytes 58613760 | tf_op jit(solution)/shard_map/sub | solution.py:147
  1862.9 12.3 copy.167
  1875.3 12.4 copy.171
  (331 shorter events, 224.4 us)
Async XLA Ops:
  7.2 15.7 copy-start
  7.2 87.3 %all-gather.17.cloned.1.call-start = ((), (), s32[]{:S(2)}) async-start(), calls=%async_computation.18 | async-start | bytes 13271040 | tf_op jit(solution)/shard_map/all_gather | solution.py:181
  7.3 15.6 copy-start.52
  22.8 152.7 %all-gather.15.cloned.1.call-start = ((), (), s32[]{:S(2)}) async-start(), calls=%async_computation.17 | async-start | bytes 2949120 | tf_op jit(solution)/shard_map/all_gather | solution.py:195
  31.4 81.2 %copy-start.49 = (s32[1536]{0:T(1024)}, s32[1536]{0:T(1024)S(1)}, u32[]{:S(2)}) copy-start(s32[1536]{0:T(1024)S(1)} %fusion.104) | copy-start | bytes 18436
  112.5 12.4 copy-start.12
  112.5 13.2 copy-start.30
  112.5 13.9 copy-start.25
  123.7 18.1 copy-start.35
  124.8 103.5 %all-gather.9.cloned.1.call-start = ((), (), s32[]{:S(2)}) async-start(), calls=%async_computation.7 | async-start | bytes 2654208 | tf_op jit(solution)/shard_map/all_gather | solution.py:184
  125.7 263.7 %all-reduce.11.cloned.1.call-start = ((), (), s32[]{:S(2)}) async-start(), calls=%async_computation.6 | async-start | bytes 9437184 | tf_op jit(solution)/shard_map/psum | solution.py:210
  151.1 64.4 %copy-start.10 = (bf16[192,768]{0,1:T(8,128)(2,1)}, bf16[192,768]{0,1:T(8,128)(2,1)S(1)}, u32[]{:S(2)}) copy-start(bf16[192,768]{0,1:T(8,128)(2,1)S(1)} %all_gather.30) | copy-start | bytes 884740
  151.8 27.5 %copy-start.19 = (f32[1536,32]{0,1:T(8,128)}, f32[1536,32]{0,1:T(8,128)S(1)}, u32[]{:S(2)}) copy-start(f32[1536,32]{0,1:T(8,128)S(1)} %get-tuple-element.486) | copy-start | bytes 589828
  151.9 27.5 %copy-start.21 = (f32[1536,32]{0,1:T(8,128)}, f32[1536,32]{0,1:T(8,128)S(1)}, u32[]{:S(2)}) copy-start(f32[1536,32]{0,1:T(8,128)S(1)} %get-tuple-element.487) | copy-start | bytes 589828
  218.5 196.3 %all-gather.11.cloned.1.call-start = ((), (), s32[]{:S(2)}) async-start(), calls=%async_computation.8 | async-start | bytes 1327104 | tf_op jit(solution)/shard_map/all_gather | solution.py:185
  219.2 373.9 %all-reduce.13.cloned.1.call-start = ((), (), s32[]{:S(2)}) async-start(), calls=%async_computation.9 | async-start | bytes 9437184 | tf_op jit(solution)/shard_map/psum | solution.py:218
  228.3 585.8 %copy-start.45 = (f32[768]{0:T(1024)}, f32[768]{0:T(1024)S(1)}, u32[]{:S(2)}) copy-start(f32[768]{0:T(1024)S(1)} %get-tuple-element.396) | copy-start | bytes 9220
  393.4 420.7 %copy-start.41 = (f32[1536]{0:T(1024)}, f32[1536]{0:T(1024)S(1)}, u32[]{:S(2)}) copy-start(f32[1536]{0:T(1024)S(1)} %broadcast_multiply_fusion.3) | copy-start | bytes 18436
  393.9 420.1 %copy-start.43 = (f32[1536]{0:T(1024)}, f32[1536]{0:T(1024)S(1)}, u32[]{:S(2)}) copy-start(f32[1536]{0:T(1024)S(1)} %fusion.101) | copy-start | bytes 18436
  421.0 382.4 %all-reduce.15.cloned.1.call-start = ((), (), s32[]{:S(2)}) async-start(), calls=%async_computation.10 | async-start | bytes 9437184 | tf_op jit(solution)/shard_map/psum | solution.py:258
  617.5 185.9 %copy-start.47 = (f32[1536]{0:T(1024)}, f32[1536]{0:T(1024)S(1)}, u32[]{:S(2)}) copy-start(f32[1536]{0:T(1024)S(1)} %negate_multiply_fusion.1) | copy-start | bytes 18436
  633.2 530.8 %all-reduce.17.cloned.1.call-start = ((), (), s32[]{:S(2)}) async-start(), calls=%async_computation.11 | async-start | bytes 9437184 | tf_op jit(solution)/shard_map/psum | solution.py:283
  821.4 163.9 %copy-start.20 = (f32[1536,32]{0,1:T(8,128)S(1)}, f32[1536,32]{0,1:T(8,128)}, u32[]{:S(2)}) copy-start(f32[1536,32]{0,1:T(8,128)} %copy-done.19) | copy-start | bytes 589828
  992.9 383.2 %reduce-scatter.11.cloned.1.call-start = ((), (), s32[]{:S(2)}) async-start(), calls=%async_computation.12 | async-start | bytes 35168256 | tf_op jit(solution)/shard_map/reduce_scatter | solution.py:292
  1187.5 7.5 copy-start.51
  1187.5 8.8 copy-start.9
  1187.5 234.4 %reduce-scatter.17.cloned.1.call-start = ((), (), s32[]{:S(2)}) async-start(), calls=%async_computation.15 | async-start | bytes 2654208 | tf_op jit(solution)/shard_map/reduce_scatter | solution.py:296
  1194.9 264.7 %reduce-scatter.21.cloned.1.call-start = ((), (), s32[]{:S(2)}) async-start(), calls=%async_computation.20 | async-start | bytes 442368
  1196.0 302.0 %reduce-scatter.19.cloned.1.call-start = ((), (), s32[]{:S(2)}) async-start(), calls=%async_computation.19 | async-start | bytes 884736
  1201.7 354.7 %reduce-scatter.15.cloned.1.call-start = ((), (), s32[]{:S(2)}) async-start(), calls=%async_computation.14 | async-start | bytes 5308416 | tf_op jit(solution)/shard_map/reduce_scatter | solution.py:295
  1217.1 385.6 %reduce-scatter.13.cloned.1.call-start = ((), (), s32[]{:S(2)}) async-start(), calls=%async_computation.13 | async-start | bytes 2654208 | tf_op jit(solution)/shard_map/reduce_scatter | solution.py:293
  1224.7 586.4 %all-gather.13.cloned.1.call-start = ((), (), s32[]{:S(2)}) async-start(), calls=%async_computation.16 | async-start | bytes 14745600 | tf_op jit(solution)/shard_map/all_gather | solution.py:302
  1611.3 67.6 %copy-start.13 = (f32[96,2,768]{2,1,0:T(2,128)S(1)}, f32[96,2,768]{2,1,0:T(2,128)}, u32[]{:S(2)}) copy-start(f32[96,2,768]{2,1,0:T(2,128)} %param.37) | copy-start | bytes 1769476
  1611.3 67.6 %copy-start.14 = (f32[96,2,768]{2,0,1:T(8,128)S(1)}, f32[96,2,768]{2,0,1:T(8,128)}, u32[]{:S(2)}) copy-start(f32[96,2,768]{2,0,1:T(8,128)} %reduce-scatter.15.cloned.1.call-done) | copy-start | bytes 1769476
  1611.3 67.6 %copy-start.31 = (f32[96,2,768]{2,1,0:T(2,128)S(1)}, f32[96,2,768]{2,1,0:T(2,128)}, u32[]{:S(2)}) copy-start(f32[96,2,768]{2,1,0:T(2,128)} %param.43) | copy-start | bytes 1769476
  1611.3 67.6 %copy-start.32 = (f32[96,2,768]{2,1,0:T(2,128)S(1)}, f32[96,2,768]{2,1,0:T(2,128)}, u32[]{:S(2)}) copy-start(f32[96,2,768]{2,1,0:T(2,128)} %param.49) | copy-start | bytes 1769476
  1624.6 58.6 %copy-start.54 = (f32[2,96]{1,0:T(2,128)S(1)}, f32[2,96]{1,0:T(2,128)}, u32[]{:S(2)}) copy-start(f32[2,96]{1,0:T(2,128)} %param.39) | copy-start | bytes 2308
  1624.6 58.6 %copy-start.55 = (f32[2,96]{1,0:T(2,128)S(1)}, f32[2,96]{1,0:T(2,128)}, u32[]{:S(2)}) copy-start(f32[2,96]{1,0:T(2,128)} %param.45) | copy-start | bytes 2308
  1624.6 58.6 %copy-start.56 = (f32[2,96]{1,0:T(2,128)S(1)}, f32[2,96]{1,0:T(2,128)}, u32[]{:S(2)}) copy-start(f32[2,96]{1,0:T(2,128)} %param.51) | copy-start | bytes 2308
  1624.6 59.2 %copy-start.36 = (f32[192,96]{1,0:T(8,128)S(1)}, f32[192,96]{1,0:T(8,128)}, u32[]{:S(2)}) copy-start(f32[192,96]{1,0:T(8,128)} %param.36) | copy-start | bytes 221188
  1624.6 60.9 %copy-start.24 = (f32[768,96]{0,1:T(8,128)S(1)}, f32[768,96]{0,1:T(8,128)}, u32[]{:S(2)}) copy-start(f32[768,96]{0,1:T(8,128)} %param.38) | copy-start | bytes 884740
  1624.6 60.9 %copy-start.27 = (f32[768,96]{0,1:T(8,128)S(1)}, f32[768,96]{0,1:T(8,128)}, u32[]{:S(2)}) copy-start(f32[768,96]{0,1:T(8,128)} %reduce-scatter.17.cloned.1.call-done) | copy-start | bytes 884740
  1624.6 60.9 %copy-start.37 = (f32[768,96]{0,1:T(8,128)S(1)}, f32[768,96]{0,1:T(8,128)}, u32[]{:S(2)}) copy-start(f32[768,96]{0,1:T(8,128)} %param.44) | copy-start | bytes 884740
  1678.9 7.7 copy-start.26
  1678.9 7.7 copy-start.28
  1678.9 7.7 copy-start.39
  1678.9 7.7 copy-start.40
  1875.3 12.4 copy-start.1
  (37 other events, 151.1 us)
Sparse Core Ops, SparseCore 0:
  22.9 71.4 all-gather.16
  125.0 50.4 all-gather.14
  178.0 27.8 all-gather.8
  218.6 170.7 all-reduce.10
  391.7 23.0 all-gather.10
  421.1 171.9 all-reduce.12
  633.3 170.0 all-reduce.14
  993.0 170.9 all-reduce.16
  1187.6 188.4 reduce-scatter.10
  1379.3 42.5 reduce-scatter.16
  1425.8 33.7 reduce-scatter.20
  1463.0 34.9 reduce-scatter.18
  1502.4 53.8 reduce-scatter.14
  1560.1 42.5 reduce-scatter.12
  1604.7 206.2 all-gather.12
where the time goes:
time: 1900 us
  waiting for transfers between devices  1240 us (65%)
  local copies, waits for them, and re-layouts  191 us (10%)
  matrix products  179 us (9%)
  other arithmetic  153 us (8%)
  blocking collectives  94.2 us (5%)
  between operations  21.7 us (1%)
    psum x1, waiting for transfers between devices, local(): lax.psum(jnp.dot(active_low, w_down, preferred_element_type=jnp.float32),...  171 us
    psum x1, waiting for transfers between devices, local(): lax.psum(contract(grad_qkv_low, w_qkv.reshape(D, -1), 1, 1), 'mp')  171 us
    psum x1, waiting for transfers between devices, local(): grad_one = grad_second + lax.psum(back_term, 'mp')  170 us
    psum x1, waiting for transfers between devices, local(): attn = lax.psum(attn_term, 'mp')  157 us
    reduce_scatter x1, waiting for transfers between devices, local(): lax.psum_scatter(grad_table, 'batch', scatter_dimension=0, tiled=True)  151 us
    all_gather x1, waiting for transfers between devices, local(): table_full = lax.all_gather(reduced[0], 'mp', axis=1, tiled=True)  123 us
    unnamed x132, local copies, waits for them, and re-layouts  102 us
    unnamed x17, waiting for transfers between devices  72.6 us
  transfers between devices with their start and end apart: 15, of which 14 were waited for; matrix products, arithmetic and copies ran while one was open for 8% of the time, Pallas kernels for 0%

commit v1 on v0

--- a/solution.py
+++ b/solution.py
@@ -13,6 +13,19 @@
 step_number = 3.0
 rates = (0.3, 0.02, 0.02, 0.02, 0.02, 0.3)
 negative = -1e30
+
+
+def part_the_heaps(k_dim, panel):
+    axis_key = "mp"
+    nodes = lax.axis_size(axis_key)
+    entries = list(map(lambda kk: (kk, (kk + 1) % nodes), range(nodes)))
+    u1 = [None] * nodes
+    u1[nodes - 1] = panel
+    for q in range(nodes - 2, -1, -1):
+        u1[q] = lax.ppermute(u1[q + 1], axis_key, entries)
+    return jnp.roll(
+        jnp.concatenate(u1, k_dim), (lax.axis_index(axis_key) + 1) * panel.shape[k_dim], k_dim
+    )
 
 
 def positions(segment_row, segment_count):
@@ -299,7 +312,7 @@
     squares = sum((jnp.sum(part * part) for part in reduced[:5])) + jnp.sum(
         reduced[5] * reduced[5]
     ) / lax.axis_size("mp")
-    table_full = lax.all_gather(reduced[0], "mp", axis=1, tiled=True)
+    table_full = part_the_heaps(1, reduced[0])
     total_squares = lax.psum(squares, ("batch", "mp"))
     grad_norm = jnp.sqrt(total_squares)
     scale = clip_limit / jnp.maximum(grad_norm, clip_limit)

time: 1900 us -> 1710 us (0.900)
  waiting for transfers between devices: 1240 us -> 1130 us
  local copies, waits for them, and re-layouts: 191 us -> 158 us
  matrix products: 179 us -> 149 us
    ppermute x0 -> x3, waiting for transfers between devices: none -> 127 us  [part_the_heaps(): u1[q] = lax.ppermute(u1[q + 1], axis_key, entries)]
    all_gather x1 -> x0, waiting for transfers between devices: 123 us -> none  [local(): table_full = lax.all_gather(reduced[0], 'mp', axis=1, tiled=True)]
    unnamed x132 -> x116, local copies, waits for them, and re-layouts: 102 us -> 26 us
    unnamed x17 -> x16, waiting for transfers between devices: 72.6 us -> 0.25 us
    reduce_scatter x1, waiting for transfers between devices: 28 us -> 0.01 us  [local(): lax.psum_scatter(grad_down, 'batch', scatter_dimension=1, tiled=True)]
    concatenate x0 -> x1, local copies, waits for them, and re-layouts: none -> 27.7 us  [part_the_heaps(): jnp.roll(jnp.concatenate(u1, k_dim), (lax.axis_index(axis_key) + 1) * pan...]
    reduce_scatter x1, waiting for transfers between devices: 56.7 us -> 35.4 us  [local(): lax.psum_scatter(grad_gu.reshape(D, 2, -1), 'batch', scatter_dimension=0,...]
  transfers between devices with their start and end apart: 15 -> 17, of which waited for: 14 -> 12; matrix products, arithmetic and copies ran while one was open for 8% -> 8% of each run, Pallas kernels for 0% -> 0%
where the time goes in v1:
time: 1710 us; the launch traced here: 1700 us
  waiting for transfers between devices  1130 us (66%)
  local copies, waits for them, and re-layouts  158 us (9%)
  matrix products  149 us (9%)
  other arithmetic  146 us (9%)
  blocking collectives  80.6 us (5%)
  between operations  21.7 us (1%)
    psum x1, waiting for transfers between devices, local(): lax.psum(jnp.dot(active_low, w_down, preferred_element_type=jnp.float32),...  171 us
    psum x1, waiting for transfers between devices, local(): lax.psum(contract(grad_qkv_low, w_qkv.reshape(D, -1), 1, 1), 'mp')  171 us
    psum x1, waiting for transfers between devices, local(): grad_one = grad_second + lax.psum(back_term, 'mp')  170 us
    reduce_scatter x1, waiting for transfers between devices, local(): lax.psum_scatter(grad_table, 'batch', scatter_dimension=0, tiled=True)  159 us
    psum x1, waiting for transfers between devices, local(): attn = lax.psum(attn_term, 'mp')  156 us
    ppermute x3, waiting for transfers between devices, part_the_heaps(): u1[q] = lax.ppermute(u1[q + 1], axis_key, entries)  127 us
    all_gather x1, waiting for transfers between devices, local(): lax.all_gather(table_cols.astype(jnp.bfloat16), 'batch', axis=0, tiled=True)  62.5 us
    reduce_scatter x1, waiting for transfers between devices, local(): lax.psum_scatter(grad_qkv.reshape(D, 3, -1), 'batch', scatter_dimension=0...  44.5 us
  transfers between devices with their start and end apart: 17, of which 12 were waited for; matrix products, arithmetic and copies ran while one was open for 8% of the time, Pallas kernels for 0%

profile of v1, /device:TPU:0, one launch (start us, length us, event | category | flops | bytes accessed | tf_op | source)
XLA Modules:
  0.0 1704.7 jit_solution(17679098862150945151)
XLA Ops:
  13.2 8.4 gather_fusion
  21.7 62.5 %all-gather.14.cloned.1.call-done = bf16[8,3816,192]{1,2,0:T(8,128)(2,1)} async-done(((bf16[1,3816,192]{1,2,0:T(8,128)(2,1)}), bf16[8,3816,192]{1,2,0:T(8,128)(2,1)}) %all-gather.14.cloned.1.call-update) | async-done | bytes 11722768 | tf_op jit(solution)/shard_map/all_gather | solution.py:194
  84.2 18.0 %copy.140 = bf16[8,3816,192]{2,1,0:T(8,128)(2,1)} copy(bf16[8,3816,192]{1,2,0:T(8,128)(2,1)} %all-gather.14.cloned.1.call-done) | data formatting | bytes 23445504 | tf_op jit(solution)/shard_map/all_gather | solution.py:194
  102.3 11.2 gather_fusion.1
  116.4 9.5 all_gather.27
  126.0 13.1 all_gather.26
  140.8 24.5 %all-gather.12.cloned.1.call-done = bf16[1536,768]{0,1:T(8,128)(2,1)} async-done(((bf16[1536,192]{0,1:T(8,128)(2,1)}), bf16[1536,768]{0,1:T(8,128)(2,1)}) %all-gather.12.cloned.1.call-update) | async-done | bytes 2359312 | tf_op jit(solution)/shard_map/all_gather | solution.py:208
  169.3 33.8 %while.31 = (s32[]{:T(128)}, bf16[3,512,3,64]{1,3,2,0:T(8,128)(2,1)}, f32[3,3,512]{2,1,0:T(4,128)S(1)}, s32[3]{0:T(128)S(1)}, s32[1536]{0:T(1024)S(1)}, /*index=...) while((s32[]{:T(128)}, ...), condition=%wide.region_6.7_spmd, body=%wide.region_3.6_spmd.sunk | while | flops 633076224 | bytes 38029576 | solution.py:105
  211.0 8.9 all-gather.2
  224.3 155.7 %all-reduce.11.cloned.1.call-done = f32[1536,768]{0,1:T(8,128)} async-done(((f32[1536,768]{0,1:T(8,128)}), f32[1536,768]{0,1:T(8,128)}) %all-reduce.11.cloned.1.call-update) | async-done | bytes 4718608 | tf_op jit(solution)/shard_map/psum | solution.py:223
  395.9 9.5 all-gather.10.cloned.1.call-done
  405.4 5.4 fusion.123
  411.8 171.2 %all-reduce.13.cloned.1.call-done = f32[1536,768]{0,1:T(8,128)} async-done(((f32[1536,768]{0,1:T(8,128)}), f32[1536,768]{0,1:T(8,128)}) %all-reduce.13.cloned.1.call-update) | async-done | bytes 4718608 | tf_op jit(solution)/shard_map/psum | solution.py:231
  591.1 9.5 all_gather.31
  607.5 6.2 multiply_bitcast_fusion
  617.2 5.5 convolution_bitcast_fusion
  623.2 169.7 %all-reduce.15.cloned.1.call-done = f32[1536,768]{0,1:T(8,128)} async-done(((f32[1536,768]{0,1:T(8,128)}), f32[1536,768]{0,1:T(8,128)}) %all-reduce.15.cloned.1.call-update) | async-done | bytes 4718608 | tf_op jit(solution)/shard_map/psum | solution.py:271
  792.9 6.2 multiply_reduce_fusion.2
  810.8 133.5 %while.32 = (s32[]{:T(128)}, f32[1,1536,3,64]{1,3,2,0:T(8,128)S(1)}, f32[1,1536,3,64]{1,3,2,0:T(8,128)S(1)}, f32[3,512,3,64]{1,0,3,2:T(4,128)}, s32[3]{0:T(128)S...) while((s32[]{:T(128)}, ...), condition=%wide.region_29.30_spmd.clone, body=%wide.region_26.29_spmd.clone.sunk | while | flops 1534130688 | bytes 138272240 | solution.py:150
  819.9 7.1 multiply_reduce_fusion.16
  827.0 9.4 multiply_convert_fusion.4
  836.4 5.8 fusion.169
  846.7 8.6 dynamic_update_slice.22
  864.4 7.1 multiply_reduce_fusion.16
  871.5 9.4 multiply_convert_fusion.4
  880.9 5.8 fusion.169
  891.2 8.6 dynamic_update_slice.22
  908.9 7.1 multiply_reduce_fusion.16
  916.0 9.4 multiply_convert_fusion.4
  925.4 5.8 fusion.169
  935.7 8.6 dynamic_update_slice.22
  955.0 171.1 %all-reduce.17.cloned.1.call-done = f32[1536,768]{0,1:T(8,128)} async-done(((f32[1536,768]{0,1:T(8,128)}), f32[1536,768]{0,1:T(8,128)}) %all-reduce.17.cloned.1.call-update) | async-done | bytes 4718608 | tf_op jit(solution)/shard_map/psum | solution.py:296
  1128.3 21.2 %scatter_custom_fusion = f32[30528,192]{1,0:T(8,128)} fusion(s32[1536]{0:T(1024)} %copy-done.44, f32[1536,192]{1,0:T(8,128)S(1)} %copy.155, f32[]{:T(128)} %constant.245.clone.1), kind=kCustom, calls=%fused_computation.51 | custom fusion | flops 294912 | bytes 23446016 | tf_op jit(solution)/shard_map/scatter-add | solution.py:301
  1151.2 5.8 fusion.73
  1158.3 5.4 convolution_bitcast_fusion.1
  1163.8 15.3 fusion.50
  1179.1 159.0 %reduce-scatter.11.cloned.1.call-done = f32[3816,192]{1,0:T(8,128)} async-done(((f32[30528,192]{1,0:T(8,128)}), f32[3816,192]{1,0:T(8,128)}) %reduce-scatter.11.cloned.1.call-update) | async-done | bytes 2930704 | tf_op jit(solution)/shard_map/reduce_scatter | solution.py:305
  1338.2 5.1 copy.156
  1344.7 66.1 %collective-permute-done = f32[3816,192]{0,1:T(8,128)S(1)} collective-permute-done((f32[3816,192]{0,1:T(8,128)}, f32[3816,192]{0,1:T(8,128)S(1)}, u32[]{:S(2)}, u32[]{:S(2)}) %collective-permute-start) | collective-permute-done | bytes 2930720 | tf_op jit(solution)/shard_map/ppermute | solution.py:25
  1410.9 5.6 fusion.63
  1416.5 61.0 %collective-permute-done.1 = f32[3816,192]{0,1:T(8,128)} collective-permute-done((f32[3816,192]{0,1:T(8,128)S(1)}, f32[3816,192]{0,1:T(8,128)}, u32[]{:S(2)}, u32[]{:S(2)}) %collective-permute-start.1) | collective-permute-done | bytes 2930720 | tf_op jit(solution)/shard_map/ppermute | solution.py:25
  1483.0 35.4 %reduce-scatter.15.cloned.1.call-done = f32[96,2,768]{2,0,1:T(8,128)} async-done(((f32[768,2,768]{2,0,1:T(8,128)}), f32[96,2,768]{2,0,1:T(8,128)}) %reduce-scatter.15.cloned.1.call-update) | async-done | bytes 589840 | tf_op jit(solution)/shard_map/reduce_scatter | solution.py:308
  1520.2 44.5 %reduce-scatter.13.cloned.1.call-done = f32[96,3,192]{2,0,1:T(8,128)} async-done(((f32[768,3,192]{2,0,1:T(8,128)}), f32[96,3,192]{2,0,1:T(8,128)}) %reduce-scatter.13.cloned.1.call-update) | async-done | bytes 221200 | tf_op jit(solution)/shard_map/reduce_scatter | solution.py:306
  1573.3 39.6 %psum.39 = f32[]{:T(128)} all-reduce(f32[]{:T(128)S(6)} %add.337), channel_id=1, replica_groups=mesh['batch'=8,'mp'=4] {'batch','mp'}, use_global_device_ids=true, to_apply=%region_46.47 | all-reduce | flops 1 | bytes 8 | tf_op jit(solution)/shard_map/psum | solution.py:316
  1628.2 5.0 copy.158
  1633.2 5.0 copy.157
  1638.2 27.7 %concatenate.42 = f32[3816,1536]{1,0:T(8,128)} concatenate(f32[3816,192]{1,0:T(8,128)} %copy.157, f32[3816,192]{1,0:T(8,128)} %copy.158, f32[3816,192]{1,0:T(8,128)} %copy.159, f32[3816,192]{1,0:T(8,128)} %reduce-scatter.11.cloned.1.call-done, f32[3816,192]{1,0:T(8,128)} %copy.157, f32[3816,192]{1,0:T(8,128)} %copy.158, f32[3816,192]{1,0:T(8,128)} %copy.159, ...), dimensions={1} | concatenate | bytes 46891008 | tf_op jit(solution)/shard_map/jit(_roll_dynamic)/concatenate | solution.py:26
  1665.9 30.8 %fusion.45 = (f32[3816,768]{1,0:T(8,128)}, f32[3816,768]{1,0:T(8,128)}, f32[3816,768]{1,0:T(8,128)}) fusion(f32[3816,768]{1,0:T(8,128)} %param.34, f32[3816,768]{1,0:T(8,128)} %param.40, f32[3816,768]{1,0:T(8,128)} %param.46, f32[]{:T(128)S(6)} %div.197, f32[3816,1536]{1,0:T(8,128)} %concatenate.42, s32[]{:T(128)S(6)} %select_n.106), kind=kLoop, calls=%fused_computation.57 | loop fusion | flops 43960320 | bytes 82059272 | tf_op jit(solution)/shard_map/sub | solution.py:160
  (322 shorter events, 175.9 us)
Async XLA Ops:
  7.2 77.0 %all-gather.14.cloned.1.call-start = ((), (), s32[]{:S(2)}) async-start(), calls=%async_computation.17 | async-start | bytes 13271040 | tf_op jit(solution)/shard_map/all_gather | solution.py:194
  13.1 152.1 %all-gather.12.cloned.1.call-start = ((), (), s32[]{:S(2)}) async-start(), calls=%async_computation.16 | async-start | bytes 2949120 | tf_op jit(solution)/shard_map/all_gather | solution.py:208
  21.7 80.6 %copy-start.44 = (s32[1536]{0:T(1024)}, s32[1536]{0:T(1024)S(1)}, u32[]{:S(2)}) copy-start(s32[1536]{0:T(1024)S(1)} %fusion.103) | copy-start | bytes 18436
  102.3 12.4 copy-start.12
  102.3 13.2 copy-start.27
  102.3 13.9 copy-start.30
  102.3 14.0 copy-start.22
  114.6 105.5 %all-gather.8.cloned.1.call-start = ((), (), s32[]{:S(2)}) async-start(), calls=%async_computation.7 | async-start | bytes 2654208 | tf_op jit(solution)/shard_map/all_gather | solution.py:197
  115.4 264.6 %all-reduce.11.cloned.1.call-start = ((), (), s32[]{:S(2)}) async-start(), calls=%async_computation.6 | async-start | bytes 9437184 | tf_op jit(solution)/shard_map/psum | solution.py:223
  140.0 28.5 %copy-start.25 = (bf16[768,3,192]{0,2,1:T(8,128)(2,1)}, bf16[768,3,192]{0,2,1:T(8,128)(2,1)S(1)}, u32[]{:S(2)}) copy-start(bf16[768,3,192]{0,2,1:T(8,128)(2,1)S(1)} %copy.143) | copy-start | bytes 2654212
  140.7 28.1 %copy-start.18 = (f32[1536,32]{0,1:T(8,128)}, f32[1536,32]{0,1:T(8,128)S(1)}, u32[]{:S(2)}) copy-start(f32[1536,32]{0,1:T(8,128)S(1)} %get-tuple-element.487) | copy-start | bytes 589828
  140.8 28.1 %copy-start.19 = (f32[1536,32]{0,1:T(8,128)}, f32[1536,32]{0,1:T(8,128)S(1)}, u32[]{:S(2)}) copy-start(f32[1536,32]{0,1:T(8,128)S(1)} %get-tuple-element.488) | copy-start | bytes 589828
  209.1 171.0 %copy-start.13 = (bf16[1536,768]{0,1:T(8,128)(2,1)S(1)}, bf16[1536,768]{0,1:T(8,128)(2,1)}, u32[]{:S(2)}) copy-start(bf16[1536,768]{0,1:T(8,128)(2,1)} %all-gather.12.cloned.1.call-done) | copy-start | bytes 7077892
  209.1 196.3 %all-gather.10.cloned.1.call-start = ((), (), s32[]{:S(2)}) async-start(), calls=%async_computation.8 | async-start | bytes 1327104 | tf_op jit(solution)/shard_map/all_gather | solution.py:198
  211.0 372.0 %all-reduce.13.cloned.1.call-start = ((), (), s32[]{:S(2)}) async-start(), calls=%async_computation.9 | async-start | bytes 9437184 | tf_op jit(solution)/shard_map/psum | solution.py:231
  220.0 583.5 %copy-start.40 = (f32[768]{0:T(1024)}, f32[768]{0:T(1024)S(1)}, u32[]{:S(2)}) copy-start(f32[768]{0:T(1024)S(1)} %get-tuple-element.396) | copy-start | bytes 9220
  383.2 7.4 copy-start.4
  383.3 420.3 %copy-start.36 = (f32[1536]{0:T(1024)}, f32[1536]{0:T(1024)S(1)}, u32[]{:S(2)}) copy-start(f32[1536]{0:T(1024)S(1)} %broadcast_multiply_fusion.2) | copy-start | bytes 18436
  383.8 419.7 %copy-start.38 = (f32[1536]{0:T(1024)}, f32[1536]{0:T(1024)S(1)}, u32[]{:S(2)}) copy-start(f32[1536]{0:T(1024)S(1)} %fusion.100) | copy-start | bytes 18436
  395.9 15.0 copy-start.16
  410.9 382.0 %all-reduce.15.cloned.1.call-start = ((), (), s32[]{:S(2)}) async-start(), calls=%async_computation.10 | async-start | bytes 9437184 | tf_op jit(solution)/shard_map/psum | solution.py:271
  607.4 185.4 %copy-start.42 = (f32[1536]{0:T(1024)}, f32[1536]{0:T(1024)S(1)}, u32[]{:S(2)}) copy-start(f32[1536]{0:T(1024)S(1)} %negate_multiply_fusion.1) | copy-start | bytes 18436
  607.5 9.7 copy-start.14
  622.7 503.4 %all-reduce.17.cloned.1.call-start = ((), (), s32[]{:S(2)}) async-start(), calls=%async_computation.11 | async-start | bytes 9437184 | tf_op jit(solution)/shard_map/psum | solution.py:296
  955.0 383.2 %reduce-scatter.11.cloned.1.call-start = ((), (), s32[]{:S(2)}) async-start(), calls=%async_computation.12 | async-start | bytes 35168256 | tf_op jit(solution)/shard_map/reduce_scatter | solution.py:305
  1149.5 7.5 copy-start.45
  1149.5 7.5 copy-start.46
  1149.5 8.8 copy-start.11
  1149.6 328.0 %reduce-scatter.17.cloned.1.call-start = ((), (), s32[]{:S(2)}) async-start(), calls=%async_computation.15 | async-start | bytes 2654208 | tf_op jit(solution)/shard_map/reduce_scatter | solution.py:309
  1157.0 322.2 %reduce-scatter.21.cloned.1.call-start = ((), (), s32[]{:S(2)}) async-start(), calls=%async_computation.19 | async-start | bytes 442368
  1158.0 323.3 %reduce-scatter.19.cloned.1.call-start = ((), (), s32[]{:S(2)}) async-start(), calls=%async_computation.18 | async-start | bytes 884736
  1163.7 354.7 %reduce-scatter.15.cloned.1.call-start = ((), (), s32[]{:S(2)}) async-start(), calls=%async_computation.14 | async-start | bytes 5308416 | tf_op jit(solution)/shard_map/reduce_scatter | solution.py:308
  1179.1 385.6 %reduce-scatter.13.cloned.1.call-start = ((), (), s32[]{:S(2)}) async-start(), calls=%async_computation.13 | async-start | bytes 2654208 | tf_op jit(solution)/shard_map/reduce_scatter | solution.py:306
  1343.2 67.6 %collective-permute-start = (f32[3816,192]{0,1:T(8,128)}, f32[3816,192]{0,1:T(8,128)S(1)}, u32[]{:S(2)}, u32[]{:S(2)}) collective-permute-start(f32[3816,192]{0,1:T(8,128)} %copy.156), channel_id=1, source_target_pairs={{0,1},{1,2},{2,3},{3,0},{4,5},{5,6},{6,7},{7,4},{8,9},{9,10},{10,1... | collective-permute-start | bytes 8792072 | tf_op jit(solution)/shard_map/ppermute | solution.py:25
  1410.9 66.7 %collective-permute-start.1 = (f32[3816,192]{0,1:T(8,128)S(1)}, f32[3816,192]{0,1:T(8,128)}, u32[]{:S(2)}, u32[]{:S(2)}) collective-permute-start(f32[3816,192]{0,1:T(8,128)S(1)} %collective-permute-done), channel_id=1, source_target_pairs={{0,1},{1,2},{2,3},{3,0},{4,5},{5,6},{6,7},{7,4},{8,9},{9,10},{10,1... | collective-permute-start | bytes 8792072 | tf_op jit(solution)/shard_map/ppermute | solution.py:25
  1477.5 155.7 %collective-permute-start.2 = (f32[3816,192]{0,1:T(8,128)}, f32[3816,192]{0,1:T(8,128)}, u32[]{:S(2)}, u32[]{:S(2)}) collective-permute-start(f32[3816,192]{0,1:T(8,128)} %collective-permute-done.1), channel_id=1, source_target_pairs={{0,1},{1,2},{2,3},{3,0},{4,5},{5,6},{6,7},{7,4},{8,9},{9,10},{10,1... | collective-permute-start | bytes 8792072 | tf_op jit(solution)/shard_map/ppermute | solution.py:25
  1570.0 49.7 %copy-start.49 = (f32[2,96]{1,0:T(2,128)S(1)}, f32[2,96]{1,0:T(2,128)}, u32[]{:S(2)}) copy-start(f32[2,96]{1,0:T(2,128)} %param.39) | copy-start | bytes 2308
  1570.0 49.7 %copy-start.50 = (f32[2,96]{1,0:T(2,128)S(1)}, f32[2,96]{1,0:T(2,128)}, u32[]{:S(2)}) copy-start(f32[2,96]{1,0:T(2,128)} %param.45) | copy-start | bytes 2308
  1570.0 49.7 %copy-start.51 = (f32[2,96]{1,0:T(2,128)S(1)}, f32[2,96]{1,0:T(2,128)}, u32[]{:S(2)}) copy-start(f32[2,96]{1,0:T(2,128)} %param.51) | copy-start | bytes 2308
  1570.0 50.3 %copy-start.31 = (f32[192,96]{1,0:T(8,128)S(1)}, f32[192,96]{1,0:T(8,128)}, u32[]{:S(2)}) copy-start(f32[192,96]{1,0:T(8,128)} %param.36) | copy-start | bytes 221188
  1570.0 52.0 %copy-start.21 = (f32[768,96]{0,1:T(8,128)S(1)}, f32[768,96]{0,1:T(8,128)}, u32[]{:S(2)}) copy-start(f32[768,96]{0,1:T(8,128)} %param.38) | copy-start | bytes 884740
  1613.7 8.3 copy-start.32
  1613.7 8.3 copy-start.33
  1613.7 10.4 copy-start.23
  1613.7 10.4 copy-start.24
  1613.7 10.4 copy-start.34
  1613.8 10.3 copy-start.35
  1665.9 30.8 %copy-start.1 = (s32[30528]{0:T(1024)S(1)}, s32[30528]{0:T(1024)}, u32[]{:S(2)}) copy-start(s32[30528]{0:T(1024)} %param.32) | copy-start | bytes 366340
  (34 other events, 136.1 us)
Sparse Core Ops, SparseCore 0:
  13.2 70.9 all-gather.13
  114.7 50.4 all-gather.11
  167.7 27.8 all-gather.7
  209.2 170.7 all-reduce.10
  382.3 23.0 all-gather.9
  411.0 171.9 all-reduce.12
  622.8 170.0 all-reduce.14
  955.1 170.9 all-reduce.16
  1149.6 188.4 reduce-scatter.10
  1341.4 42.4 reduce-scatter.16
  1387.8 33.8 reduce-scatter.20
  1425.0 34.9 reduce-scatter.18
  1464.4 53.9 reduce-scatter.14
  1522.1 42.4 reduce-scatter.12
